TPU v7x, 32 devices: a whole 2x2x4 slice. The times are simulated.
32 devices in a mesh: layer: 2 (over x), feat: 4 (over z), tok: 4 (over y, core).
Axes of the slice: x: 2, y: 2, z: 4, core: 2. Of those that a mesh axis runs over, the one named last changes fastest.
Arguments:
- resid: bfloat16 [2, 1024, 2304], P('layer', 'tok', 'feat'), may hold values from -6 to 6
- norm_gain: bfloat16 [2, 2304], P('layer', 'feat'), may hold values from 0.5 to 2
- prev_codes: bfloat16 [1024, 16384], P('tok', 'feat'), may hold values from 0 to 1.5
- feature_mask: int32 [2, 8, 128], P('layer', 'tok', 'feat'), may hold values 0 or 1
- w_gate: bfloat16 [2, 2304, 9216], P('layer', 'tok', 'feat'), may hold values from -0.125 to 0.125
- w_up: bfloat16 [2, 2304, 9216], P('layer', 'tok', 'feat'), may hold values from -0.125 to 0.125
- w_down: bfloat16 [2, 9216, 2304], P('layer', 'feat', 'tok'), may hold values from -0.0625 to 0.0625
- enc_weight: bfloat16 [2, 2304, 16384], P('layer', 'tok', 'feat'), may hold values from -0.125 to 0.125
- enc_bias: float32 [2, 16384], P('layer', 'feat'), may hold values from -3 to 3
- dec_own: bfloat16 [2, 16384, 2304], P('layer', 'feat', 'tok'), may hold values from -0.046875 to 0.046875
- dec_prev: bfloat16 [2, 16384, 2304], P('layer', 'feat', 'tok'), may hold values from -0.046875 to 0.046875
Outputs:
- grad_enc: float32 [2, 2304, 16384], P('layer', 'tok', 'feat')
- grad_bias: float32 [2, 16384], P('layer', 'feat')
- grad_own: float32 [2, 16384, 2304], P('layer', 'feat', 'tok')
- grad_prev: float32 [2, 16384, 2304], P('layer', 'feat', 'tok')
All inputs are finite; a program needn't handle non-finite values. No bound on the sum of `feature_mask` on one device may be relied on, other than what follows from the above.
Results may differ from a plain program's by a relative error of at most 0.0063.
Values may be sent and summed in bfloat16 or wider, within the bound.
A program may use at most 256 MiB of HBM per device.

v0:
```python
import math
import jax
import jax.numpy as jnp
from jax import lax
from jax.sharding import PartitionSpec as P

TILE = 128
TBLK = 128


def passed_along(value, axis, steps):
    count = lax.axis_size(axis)
    leading, last = (max(0, -steps), min(count, count - steps))
    return lax.ppermute(value, axis, [(source, source + steps) for source in range(leading, last)])


def block_keep(block_mask, height, breadth):
    blocks = block_mask.astype(jnp.float32)
    spread = jnp.broadcast_to(
        blocks[:, None, :, None], (blocks.shape[0], TBLK, blocks.shape[1], TILE)
    )
    return spread.reshape(height, breadth)


def local(
    resid,
    norm_gain,
    prev_codes,
    feature_mask,
    w_gate,
    w_up,
    w_down,
    enc_weight,
    enc_bias,
    dec_own,
    dec_prev,
):
    gathered, gains = (
        lax.all_gather(resid[0], "feat", axis=1, tiled=True),
        lax.all_gather(norm_gain, "feat", axis=1, tiled=True),
    )
    stream = gathered.astype(jnp.float32)
    normed = (
        stream
        * lax.rsqrt(jnp.mean(stream * stream, axis=1, keepdims=True) + 1e-06)
        * gains[0].astype(jnp.float32)
    ).astype(jnp.bfloat16)
    height = normed.shape[0]
    feat_local = enc_weight.shape[2]
    segments = (
        lax.all_gather(w_gate[0], "tok", axis=0, tiled=True),
        lax.all_gather(w_up[0], "tok", axis=0, tiled=True),
        lax.all_gather(enc_weight[0], "tok", axis=0, tiled=True),
    )
    gate_sum, up_sum, enc_sum = tuple(
        (jnp.dot(normed, segment, preferred_element_type=jnp.float32) for segment in segments)
    )
    hidden = (jax.nn.gelu(gate_sum, approximate=True) * up_sum).astype(jnp.bfloat16)
    preact = enc_sum + enc_bias[0]
    active = jnp.maximum(preact, 0.0)
    keeper = block_keep(feature_mask[0], height, feat_local)
    codes = (active * active * keeper).astype(jnp.bfloat16)
    shifted = passed_along(codes, "layer", 1)
    source = jnp.where(lax.axis_index("layer") == 0, prev_codes, shifted)
    own_full, prev_full = (
        lax.all_gather(dec_own[0], "tok", axis=1, tiled=True),
        lax.all_gather(dec_prev[0], "tok", axis=1, tiled=True),
    )
    partial_value = (
        jnp.dot(codes, own_full, preferred_element_type=jnp.float32)
        + jnp.dot(source, prev_full, preferred_element_type=jnp.float32)
        - jnp.dot(
            hidden,
            lax.all_gather(w_down[0], "tok", axis=1, tiled=True),
            preferred_element_type=jnp.float32,
        )
    )
    error = lax.psum(partial_value, "feat").astype(jnp.bfloat16)
    own_back = jnp.dot(error, own_full.T, preferred_element_type=jnp.float32)
    prev_back = jnp.dot(error, prev_full.T, preferred_element_type=jnp.float32)
    later = passed_along(prev_back.astype(jnp.bfloat16), "layer", -1).astype(prev_back.dtype)
    back = own_back + later
    factor = 1.0 / math.sqrt(height * lax.axis_size("tok"))
    pregrad = (back * keeper * (2.0 * active) * factor).astype(jnp.bfloat16)
    normed_cols = lax.all_to_all(normed, "tok", split_axis=1, concat_axis=0, tiled=True)
    error_cols = lax.all_to_all(error, "tok", split_axis=1, concat_axis=0, tiled=True)
    codes_all, source_all = (
        lax.all_gather(codes, "tok", axis=0, tiled=True),
        lax.all_gather(source, "tok", axis=0, tiled=True),
    )
    pregrad_all = lax.all_gather(pregrad, "tok", axis=0, tiled=True)
    grad_enc = jnp.dot(normed_cols.T, pregrad_all, preferred_element_type=jnp.float32)
    grad_bias = jnp.sum(pregrad_all.astype(jnp.float32), axis=0)
    grad_own = jnp.dot(codes_all.T, error_cols, preferred_element_type=jnp.float32) * factor
    grad_prev = jnp.dot(source_all.T, error_cols, preferred_element_type=jnp.float32) * factor
    return (grad_enc[None], grad_bias[None], grad_own[None], grad_prev[None])


def solution(mesh):
    in_specs = (
        P("layer", "tok", "feat"),
        P("layer", "feat"),
        P("tok", "feat"),
        P("layer", "tok", "feat"),
        P("layer", "tok", "feat"),
        P("layer", "tok", "feat"),
        P("layer", "feat", "tok"),
        P("layer", "tok", "feat"),
        P("layer", "feat"),
        P("layer", "feat", "tok"),
        P("layer", "feat", "tok"),
    )
    out_specs = (
        P("layer", "tok", "feat"),
        P("layer", "feat"),
        P("layer", "feat", "tok"),
        P("layer", "feat", "tok"),
    )
    return jax.shard_map(local, mesh=mesh, in_specs=in_specs, out_specs=out_specs, check_vma=False)
```

profile of v0, /device:TPU:0, one launch (start us, length us, event | category | flops | bytes accessed | tf_op | source)
XLA Modules:
  0.0 905.5 jit_solution(4202386493531622728)
XLA Ops:
  13.5 14.1 %all-reduce = bf16[2304]{0:T(1024)(128)(2,1)S(1)} all-reduce(bf16[2304]{0:T(1024)(128)(2,1)S(1)} %dynamic-update-slice), channel_id=1, replica_groups=mesh['layer'=2,'feat'=4,'tok'=4] {'feat'}, use_global_device_ids=true, to_apply=%add | all-reduce | flops 2304 | bytes 9216
  27.6 15.1 %all-gather.24.cloned.1.call-done = bf16[1,256,2304]{1,2,0:T(8,128)(2,1)} async-done(((bf16[1,256,576]{1,2,0:T(8,128)(2,1)}), bf16[1,256,2304]{1,2,0:T(8,128)(2,1)}) %all-gather.24.cloned.1.call-update) | async-done | bytes 1179664 | tf_op jit(solution)/shard_map/all_gather | solution.py:39
  47.0 116.6 %all-gather.26.cloned.1.call-done = bf16[1,2304,4096]{2,1,0:T(8,128)(2,1)} async-done(((bf16[1,576,4096]{2,1,0:T(8,128)(2,1)}), bf16[1,2304,4096]{2,1,0:T(8,128)(2,1)}) %all-gather.26.cloned.1.call-update) | async-done | bytes 18874384 | tf_op jit(solution)/shard_map/all_gather | solution.py:53
  164.2 16.5 %fusion.25 = (bf16[256,4096]{1,0:T(8,128)(2,1)}, f32[256,4096]{1,0:T(8,128)}) fusion(f32[32,8,32,128]{3,2,1,0:T(8,128)S(1)} %bitcast.93, f32[4096]{0:T(1024)S(1)} %bitcast.100, bf16[256,2304]{0,1:T(8,128)(2,1)} %fusion.43, bf16[1,2304,4096]{2,1,0:T(8,128)(2,1)} %all-gather.26.cloned.1.call-done), kind=kOutput, calls=%fused_computation.25 | convolution fusion | flops 4837081088 | bytes 30556160 | tf_op jit(solution)/shard_map/dot_general | solution.py:56
  180.8 4.7 collective-permute-start
  185.5 50.6 %all-gather.32.cloned.1.call-done = bf16[1,2304,2304]{2,1,0:T(8,128)(2,1)} async-done(((bf16[1,576,2304]{2,1,0:T(8,128)(2,1)}), bf16[1,2304,2304]{2,1,0:T(8,128)(2,1)}) %all-gather.32.cloned.1.call-update) | async-done | bytes 10616848 | tf_op jit(solution)/shard_map/all_gather | solution.py:51
  236.1 9.3 %fusion.50 = f32[256,2304]{1,0:T(8,128)} fusion(bf16[256,2304]{0,1:T(8,128)(2,1)} %fusion.43, bf16[1,2304,2304]{2,1,0:T(8,128)(2,1)} %all-gather.32.cloned.1.call-done), kind=kOutput, calls=%fused_computation.45 | convolution fusion | flops 2722627584 | bytes 14155776 | tf_op jit(solution)/shard_map/dot_general | solution.py:56
  247.2 110.3 %all-gather.28.cloned.1.call-done = bf16[1,4096,2304]{1,2,0:T(8,128)(2,1)} async-done(((bf16[1,4096,576]{1,2,0:T(8,128)(2,1)}), bf16[1,4096,2304]{1,2,0:T(8,128)(2,1)}) %all-gather.28.cloned.1.call-update) | async-done | bytes 18874384 | tf_op jit(solution)/shard_map/all_gather | solution.py:66
  357.5 10.4 %fusion.6 = f32[256,2304]{1,0:T(8,128)} fusion(bf16[256,4096]{1,0:T(8,128)(2,1)S(1)} %copy-done.2, bf16[1,4096,2304]{1,2,0:T(8,128)(2,1)} %all-gather.28.cloned.1.call-done), kind=kOutput, calls=%fused_computation.6 | convolution fusion | flops 4831838208 | bytes 23330816 | tf_op jit(solution)/shard_map/dot_general | solution.py:70
  368.0 111.0 %all-gather.30.cloned.1.call-done = bf16[1,4096,2304]{1,2,0:T(8,128)(2,1)} async-done(((bf16[1,4096,576]{1,2,0:T(8,128)(2,1)}), bf16[1,4096,2304]{1,2,0:T(8,128)(2,1)}) %all-gather.30.cloned.1.call-update) | async-done | bytes 18874384 | tf_op jit(solution)/shard_map/all_gather | solution.py:67
  479.0 11.7 %fusion.35 = f32[256,2304]{1,0:T(8,128)} fusion(f32[256,2304]{1,0:T(8,128)} %fusion.6, bf16[256,4096]{1,0:T(8,128)(2,1)} %broadcast_select_fusion, bf16[1,4096,2304]{1,2,0:T(8,128)(2,1)} %all-gather.30.cloned.1.call-done), kind=kOutput, calls=%fused_computation.31 | convolution fusion | flops 4832428032 | bytes 25690112 | tf_op jit(solution)/shard_map/dot_general | solution.py:71
  490.7 60.7 %all-gather.34.cloned.1.call-done = bf16[1,2304,2304]{2,1,0:T(8,128)(2,1)} async-done(((bf16[1,576,2304]{2,1,0:T(8,128)(2,1)}), bf16[1,2304,2304]{2,1,0:T(8,128)(2,1)}) %all-gather.34.cloned.1.call-update) | async-done | bytes 10616848 | tf_op jit(solution)/shard_map/all_gather | solution.py:52
  551.3 72.5 %all-gather.36.cloned.1.call-done = bf16[1,2304,2304]{1,2,0:T(8,128)(2,1)} async-done(((bf16[1,2304,576]{1,2,0:T(8,128)(2,1)}), bf16[1,2304,2304]{1,2,0:T(8,128)(2,1)}) %all-gather.36.cloned.1.call-update) | async-done | bytes 10616848 | tf_op jit(solution)/shard_map/all_gather | solution.py:74
  623.9 15.3 %fusion.32 = f32[256,2304]{1,0:T(8,128)S(1)} fusion(f32[256,2304]{1,0:T(8,128)} %fusion.35, bf16[1,2304,2304]{1,2,0:T(8,128)(2,1)} %all-gather.36.cloned.1.call-done, f32[256,2304]{1,0:T(8,128)} %fusion.50, bf16[256,2304]{0,1:T(8,128)(2,1)} %fusion.43, bf16[1,2304,2304]{2,1,0:T(8,128)(2,1)} %all-gather.34.cloned.1.call-done), kind=kOutput, calls=%fused_computation.30 | convolution fusion | flops 5437587456 | bytes 29491200 | tf_op jit(solution)/shard_map/dot_general | solution.py:72
  639.2 87.3 %all-reduce.2 = bf16[256,2304]{1,0:T(8,128)(2,1)S(1)} all-reduce(f32[256,2304]{1,0:T(8,128)S(1)} %fusion.32), channel_id=1, replica_groups=mesh['layer'=2,'feat'=4,'tok'=4] {'feat'}, use_global_device_ids=true, to_apply=%region_1.2 | all-reduce | flops 589824 | bytes 3538944 | tf_op jit(solution)/shard_map/psum | solution.py:78
  726.5 10.1 %fusion.22 = bf16[256,4096]{1,0:T(8,128)(2,1)S(1)} fusion(bf16[256,2304]{1,0:T(8,128)(2,1)S(1)} %all-reduce.2, bf16[1,4096,2304]{1,2,0:T(8,128)(2,1)} %all-gather.30.cloned.1.call-done), kind=kOutput, calls=%fused_computation.22 | convolution fusion | flops 4832886784 | bytes 22151168 | tf_op jit(solution)/shard_map/dot_general | solution.py:80
  737.9 46.5 %collective-permute-done.1 = bf16[256,4096]{1,0:T(8,128)(2,1)S(1)} collective-permute-done((bf16[256,4096]{1,0:T(8,128)(2,1)S(1)}, bf16[256,4096]{1,0:T(8,128)(2,1)S(1)}, u32[]{:S(2)}, u32[]{:S(2)}) %collective-permute-start.1) | collective-permute-done | bytes 2097184 | tf_op jit(solution)/shard_map/ppermute | solution.py:14
  784.4 16.2 %fusion.28 = bf16[256,4096]{1,0:T(8,128)(2,1)} fusion(f32[256,4096]{1,0:T(8,128)S(1)} %copy-done.4, bf16[256,4096]{1,0:T(8,128)(2,1)S(1)} %collective-permute-done.1, f32[32,8,32,128]{3,2,1,0:T(8,128)S(1)} %bitcast.94, bf16[256,2304]{1,0:T(8,128)(2,1)S(1)} %all-reduce.2, bf16[1,4096,2304]{1,2,0:T(8,128)(2,1)} %all-gather.28.cloned.1.call-done), kind=kOutput, calls=%fused_computation.28 | convolution fusion | flops 4839178240 | bytes 32636928 | tf_op jit(solution)/shard_map/dot_general | solution.py:79
  805.7 25.4 %all-to-all-done = bf16[256,4,576]{0,2,1:T(8,128)(2,1)S(1)} async-done(((bf16[256,4,576]{0,2,1:T(8,128)(2,1)}), bf16[256,4,576]{0,2,1:T(8,128)(2,1)S(1)}, u32[]{:S(2)}, u32[]{:S(2)}) %all-to-all-start) | async-done | bytes 1179680 | tf_op jit(solution)/shard_map/all_to_all | solution.py:85
  835.0 28.4 %all-to-all-done.1 = bf16[256,4,576]{0,2,1:T(8,128)(2,1)S(1)} async-done(((bf16[256,4,576]{0,2,1:T(8,128)(2,1)}), bf16[256,4,576]{0,2,1:T(8,128)(2,1)S(1)}, u32[]{:S(2)}, u32[]{:S(2)}) %all-to-all-start.1) | async-done | bytes 1179680 | tf_op jit(solution)/shard_map/all_to_all | solution.py:86
  863.7 10.9 %multiply_bitcast_fusion.1 = f32[1,4096,576]{1,2,0:T(8,128)} fusion(bf16[1024,576]{0,1:T(8,128)(2,1)S(1)} %bitcast.98, bf16[1024,4096]{1,0:T(8,128)(2,1)} %all-gather.20.cloned.1.call-done), kind=kOutput, calls=%fused_computation.18 | convolution fusion | flops 4834197504 | bytes 19005440 | tf_op jit(solution)/shard_map/dot_general | solution.py:94
  874.5 10.8 %multiply_bitcast_fusion = f32[1,4096,576]{1,2,0:T(8,128)} fusion(bf16[1024,576]{0,1:T(8,128)(2,1)S(1)} %bitcast.99, bf16[1024,4096]{1,0:T(8,128)(2,1)} %all-gather.22.cloned.1.call-done), kind=kOutput, calls=%fused_computation.17 | convolution fusion | flops 4834197504 | bytes 19005440 | tf_op jit(solution)/shard_map/dot_general | solution.py:95
  885.4 5.3 convert_reduce_fusion
  891.1 7.5 convolution_bitcast_fusion
  (61 shorter events, 23.0 us)
Async XLA Ops:
  7.2 35.6 %all-gather.24.cloned.1.call-start = ((), (), s32[]{:S(2)}) async-start(), calls=%async_computation.5 | async-start | bytes 1474560 | tf_op jit(solution)/shard_map/all_gather | solution.py:39
  7.9 155.7 %all-gather.26.cloned.1.call-start = ((), (), s32[]{:S(2)}) async-start(), calls=%async_computation.6 | async-start | bytes 23592960 | tf_op jit(solution)/shard_map/all_gather | solution.py:53
  8.6 227.4 %all-gather.32.cloned.1.call-start = ((), (), s32[]{:S(2)}) async-start(), calls=%async_computation.9 | async-start | bytes 13271040 | tf_op jit(solution)/shard_map/all_gather | solution.py:51
  9.4 348.2 %all-gather.28.cloned.1.call-start = ((), (), s32[]{:S(2)}) async-start(), calls=%async_computation.7 | async-start | bytes 23592960 | tf_op jit(solution)/shard_map/all_gather | solution.py:66
  10.0 469.0 %all-gather.30.cloned.1.call-start = ((), (), s32[]{:S(2)}) async-start(), calls=%async_computation.8 | async-start | bytes 23592960 | tf_op jit(solution)/shard_map/all_gather | solution.py:67
  10.5 1.4 copy-start.9
  10.6 2.7 copy-start.7
  10.6 17.0 %copy-start.8 = (s32[1,2,32]{2,1,0:T(2,128)S(1)}, s32[1,2,32]{2,1,0:T(2,128)}, u32[]{:S(2)}) copy-start(s32[1,2,32]{2,1,0:T(2,128)} %param.14) | copy-start | bytes 772
  10.6 540.8 %all-gather.34.cloned.1.call-start = ((), (), s32[]{:S(2)}) async-start(), calls=%async_computation.10 | async-start | bytes 13271040 | tf_op jit(solution)/shard_map/all_gather | solution.py:52
  11.2 612.7 %all-gather.36.cloned.1.call-start = ((), (), s32[]{:S(2)}) async-start(), calls=%async_computation.11 | async-start | bytes 13271040 | tf_op jit(solution)/shard_map/all_gather | solution.py:74
  11.9 851.7 %all-gather.20.cloned.1.call-start = ((), (), s32[]{:S(2)}) async-start(), calls=%async_computation.3 | async-start | bytes 10485760 | tf_op jit(solution)/shard_map/all_gather | solution.py:88
  47.0 117.2 %copy-start.6 = (f32[1,4096]{1,0:T(1,128)S(1)}, f32[1,4096]{1,0:T(1,128)}, u32[]{:S(2)}) copy-start(f32[1,4096]{1,0:T(1,128)} %param.19) | copy-start | bytes 49156
  164.2 16.5 %copy-start = (f32[2,128,32,128]{3,2,1,0:T(8,128)}, f32[2,128,32,128]{3,2,1,0:T(8,128)S(1)}, u32[]{:S(2)}) copy-start(f32[2,128,32,128]{3,2,1,0:T(8,128)S(1)} %broadcast_in_dim.20) | copy-start | bytes 12582916
  180.7 693.8 %all-gather.22.cloned.1.call-start = ((), (), s32[]{:S(2)}) async-start(), calls=%async_computation.4 | async-start | bytes 10485760 | tf_op jit(solution)/shard_map/all_gather | solution.py:89
  180.8 64.6 %collective-permute-start = (bf16[256,4096]{1,0:T(8,128)(2,1)}, bf16[256,4096]{1,0:T(8,128)(2,1)}, u32[]{:S(2)}, u32[]{:S(2)}) collective-permute-start(bf16[256,4096]{1,0:T(8,128)(2,1)} %get-tuple-element.4), channel_id=1, source_target_pairs={{0,16},{1,17},{2,18},{3,19},{4,20},{5,21},{6,22},{7,23},{8,24},{9,... | collective-permute-start | bytes 6291464 | tf_op jit(solution)/shard_map/ppermute | solution.py:14
  236.1 9.3 %copy-start.5 = (bf16[256,4096]{1,0:T(8,128)(2,1)S(1)}, bf16[256,4096]{1,0:T(8,128)(2,1)}, u32[]{:S(2)}) copy-start(bf16[256,4096]{1,0:T(8,128)(2,1)} %param.13) | copy-start | bytes 6291460
  245.4 112.1 %copy-start.2 = (bf16[256,4096]{1,0:T(8,128)(2,1)S(1)}, bf16[256,4096]{1,0:T(8,128)(2,1)}, u32[]{:S(2)}) copy-start(bf16[256,4096]{1,0:T(8,128)(2,1)} %get-tuple-element.4) | copy-start | bytes 6291460
  247.0 638.4 %all-gather.18.cloned.1.call-start = ((), (), s32[]{:S(2)}) async-start(), calls=%async_computation.2 | async-start | bytes 10485760 | tf_op jit(solution)/shard_map/all_gather | solution.py:91
  726.5 57.9 %copy-start.1 = (f32[2,128,32,128]{3,2,1,0:T(8,128)S(1)}, f32[2,128,32,128]{3,2,1,0:T(8,128)}, u32[]{:S(2)}) copy-start(f32[2,128,32,128]{3,2,1,0:T(8,128)} %copy-done) | copy-start | bytes 12582916
  726.5 57.9 %copy-start.4 = (f32[256,4096]{1,0:T(8,128)S(1)}, f32[256,4096]{1,0:T(8,128)}, u32[]{:S(2)}) copy-start(f32[256,4096]{1,0:T(8,128)} %get-tuple-element.5) | copy-start | bytes 12582916
  736.6 47.8 %collective-permute-start.1 = (bf16[256,4096]{1,0:T(8,128)(2,1)S(1)}, bf16[256,4096]{1,0:T(8,128)(2,1)S(1)}, u32[]{:S(2)}, u32[]{:S(2)}) collective-permute-start(bf16[256,4096]{1,0:T(8,128)(2,1)S(1)} %fusion.22), channel_id=1, source_target_pairs={{16,0},{17,1},{18,2},{19,3},{20,4},{21,5},{22,6},{23,7},{24,8},{25... | collective-permute-start | bytes 6291464 | tf_op jit(solution)/shard_map/ppermute | solution.py:14
  800.7 30.4 %all-to-all-start = ((bf16[256,4,576]{0,2,1:T(8,128)(2,1)}), bf16[256,4,576]{0,2,1:T(8,128)(2,1)S(1)}, u32[]{:S(2)}, u32[]{:S(2)}) async-start(bf16[256,4,576]{0,2,1:T(8,128)(2,1)} %bitcast.3), calls=%async_computation | async-start | bytes 2359296 | tf_op jit(solution)/shard_map/all_to_all | solution.py:85
  831.1 32.4 %all-to-all-start.1 = ((bf16[256,4,576]{0,2,1:T(8,128)(2,1)}), bf16[256,4,576]{0,2,1:T(8,128)(2,1)S(1)}, u32[]{:S(2)}, u32[]{:S(2)}) async-start(bf16[256,4,576]{0,2,1:T(8,128)(2,1)} %bitcast.15), calls=%async_computation.1 | async-start | bytes 2359296 | tf_op jit(solution)/shard_map/all_to_all | solution.py:86
  885.4 5.8 copy-start.3
Sparse Core Ops, SparseCore 0:
  9.5 33.1 all-gather.23
  44.3 119.2 all-gather.25
  165.1 70.9 all-gather.31
  237.5 119.9 all-gather.27
  359.0 119.9 all-gather.29
  480.4 70.9 all-gather.33
  552.9 70.9 all-gather.35
  625.4 58.2 all-gather.19
  685.3 58.2 all-gather.21
  800.8 78.5 all-gather.17
where the time goes:
time: 906 us; the launch traced here: 905 us
  waiting for transfers between devices  642 us (71%)
  matrix products  119 us (13%)
  blocking collectives  101 us (11%)
  between operations  15 us (2%)
  starting transfers between devices  13.9 us (2%)
  other arithmetic  11.2 us (1%)
    all_gather x1, waiting for transfers between devices, local(): lax.all_gather(enc_weight[0], 'tok', axis=0, tiled=True)  117 us
    all_gather x1, waiting for transfers between devices, local(): lax.all_gather(dec_prev[0], 'tok', axis=1, tiled=True)  111 us
    all_gather x1, waiting for transfers between devices, local(): lax.all_gather(dec_own[0], 'tok', axis=1, tiled=True)  110 us
    psum x1, blocking collectives, local(): error = lax.psum(partial_value, 'feat').astype(jnp.bfloat16)  87.3 us
    all_gather x1, waiting for transfers between devices, local(): lax.all_gather(w_down[0], 'tok', axis=1, tiled=True)  72.5 us
    all_gather x1, waiting for transfers between devices, local(): lax.all_gather(w_up[0], 'tok', axis=0, tiled=True)  60.7 us
    all_gather x1, waiting for transfers between devices, local(): lax.all_gather(w_gate[0], 'tok', axis=0, tiled=True)  50.6 us
    ppermute x2, waiting for transfers between devices, passed_along(): lax.ppermute(value, axis, [(source, source + steps) for source in range(l...  46.5 us
  transfers between devices with their start and end apart: 14, of which 10 were waited for; matrix products, arithmetic and copies ran while one was open for 13% of the time, Pallas kernels for 0%

commit v1 on v0

--- a/solution.py
+++ b/solution.py
@@ -6,6 +6,11 @@
 
 TILE = 128
 TBLK = 128
+
+
+def gather_and_add(array, axis):
+    parts = lax.all_gather(array, axis)
+    return jnp.sum(parts, axis=0)
 
 
 def passed_along(value, axis, steps):
@@ -75,7 +80,7 @@
             preferred_element_type=jnp.float32,
         )
     )
-    error = lax.psum(partial_value, "feat").astype(jnp.bfloat16)
+    error = gather_and_add(partial_value, "feat").astype(jnp.bfloat16)
     own_back = jnp.dot(error, own_full.T, preferred_element_type=jnp.float32)
     prev_back = jnp.dot(error, prev_full.T, preferred_element_type=jnp.float32)
     later = passed_along(prev_back.astype(jnp.bfloat16), "layer", -1).astype(prev_back.dtype)

time: 906 us -> 1030 us (1.14)
  waiting for transfers between devices: 642 us -> 843 us
  blocking collectives: 101 us -> 14.1 us
    all_gather x0 -> x1, waiting for transfers between devices: none -> 166 us  [gather_and_add(): parts = lax.all_gather(array, axis)]
    psum x1 -> x0, blocking collectives: 87.3 us -> none  [local(): error = lax.psum(partial_value, 'feat').astype(jnp.bfloat16)]
    all_gather x1, waiting for transfers between devices: 0.01 us -> 39 us  [local(): pregrad_all = lax.all_gather(pregrad, 'tok', axis=0, tiled=True)]
  transfers between devices with their start and end apart: 14 -> 15, of which waited for: 10 -> 12; matrix products, arithmetic and copies ran while one was open for 13% -> 11% of each run, Pallas kernels for 0% -> 0%
where the time goes in v1:
time: 1030 us
  waiting for transfers between devices  843 us (82%)
  matrix products  125 us (12%)
  other arithmetic  16.4 us (2%)
  between operations  14.7 us (1%)
  blocking collectives  14.1 us (1%)
  starting transfers between devices  13.8 us (1%)
    all_gather x1, waiting for transfers between devices, gather_and_add(): parts = lax.all_gather(array, axis)  166 us
    all_gather x1, waiting for transfers between devices, local(): lax.all_gather(enc_weight[0], 'tok', axis=0, tiled=True)  117 us
    all_gather x1, waiting for transfers between devices, local(): lax.all_gather(dec_own[0], 'tok', axis=1, tiled=True)  112 us
    all_gather x1, waiting for transfers between devices, local(): lax.all_gather(dec_prev[0], 'tok', axis=1, tiled=True)  109 us
    all_gather x1, waiting for transfers between devices, local(): lax.all_gather(w_down[0], 'tok', axis=1, tiled=True)  72.5 us
    all_gather x1, waiting for transfers between devices, local(): lax.all_gather(w_up[0], 'tok', axis=0, tiled=True)  61 us
    all_gather x1, waiting for transfers between devices, local(): lax.all_gather(w_gate[0], 'tok', axis=0, tiled=True)  51.1 us
    ppermute x2, waiting for transfers between devices, passed_along(): lax.ppermute(value, axis, [(source, source + steps) for source in range(l...  48.2 us
  transfers between devices with their start and end apart: 15, of which 12 were waited for; matrix products, arithmetic and copies ran while one was open for 11% of the time, Pallas kernels for 0%

profile of v1, /device:TPU:0, one launch (start us, length us, event | category | flops | bytes accessed | tf_op | source)
XLA Modules:
  0.0 1030.3 jit_solution(12065468270862980284)
XLA Ops:
  13.5 14.1 %all-reduce = bf16[2304]{0:T(1024)(128)(2,1)S(1)} all-reduce(bf16[2304]{0:T(1024)(128)(2,1)S(1)} %dynamic-update-slice), channel_id=1, replica_groups=mesh['layer'=2,'feat'=4,'tok'=4] {'feat'}, use_global_device_ids=true, to_apply=%add | all-reduce | flops 2304 | bytes 9216
  27.6 15.1 %all-gather.26.cloned.1.call-done = bf16[1,256,2304]{1,2,0:T(8,128)(2,1)} async-done(((bf16[1,256,576]{1,2,0:T(8,128)(2,1)}), bf16[1,256,2304]{1,2,0:T(8,128)(2,1)}) %all-gather.26.cloned.1.call-update) | async-done | bytes 1179664 | tf_op jit(solution)/shard_map/all_gather | solution.py:44
  47.0 116.5 %all-gather.28.cloned.1.call-done = bf16[1,2304,4096]{2,1,0:T(8,128)(2,1)} async-done(((bf16[1,576,4096]{2,1,0:T(8,128)(2,1)}), bf16[1,2304,4096]{2,1,0:T(8,128)(2,1)}) %all-gather.28.cloned.1.call-update) | async-done | bytes 18874384 | tf_op jit(solution)/shard_map/all_gather | solution.py:58
  164.2 16.1 %fusion.25 = (bf16[256,4096]{1,0:T(8,128)(2,1)S(1)}, f32[256,4096]{1,0:T(8,128)}) fusion(f32[32,8,32,128]{3,2,1,0:T(8,128)S(1)} %bitcast.94, f32[4096]{0:T(1024)S(1)} %bitcast.102, bf16[256,2304]{0,1:T(8,128)(2,1)} %fusion.43, bf16[1,2304,4096]{2,1,0:T(8,128)(2,1)} %all-gather.28.cloned.1.call-done), kind=kOutput, calls=%fused_computation.25 | convolution fusion | flops 4837081088 | bytes 30556160 | tf_op jit(solution)/shard_map/dot_general | solution.py:61
  185.0 51.1 %all-gather.34.cloned.1.call-done = bf16[1,2304,2304]{2,1,0:T(8,128)(2,1)} async-done(((bf16[1,576,2304]{2,1,0:T(8,128)(2,1)}), bf16[1,2304,2304]{2,1,0:T(8,128)(2,1)}) %all-gather.34.cloned.1.call-update) | async-done | bytes 10616848 | tf_op jit(solution)/shard_map/all_gather | solution.py:56
  236.1 9.2 fusion.50
  245.3 112.2 %all-gather.30.cloned.1.call-done = bf16[1,4096,2304]{1,2,0:T(8,128)(2,1)} async-done(((bf16[1,4096,576]{1,2,0:T(8,128)(2,1)}), bf16[1,4096,2304]{1,2,0:T(8,128)(2,1)}) %all-gather.30.cloned.1.call-update) | async-done | bytes 18874384 | tf_op jit(solution)/shard_map/all_gather | solution.py:71
  357.5 10.4 %fusion.6 = f32[256,2304]{1,0:T(8,128)} fusion(bf16[256,4096]{1,0:T(8,128)(2,1)S(1)} %get-tuple-element.4, bf16[1,4096,2304]{1,2,0:T(8,128)(2,1)} %all-gather.30.cloned.1.call-done), kind=kOutput, calls=%fused_computation.6 | convolution fusion | flops 4831838208 | bytes 23330816 | tf_op jit(solution)/shard_map/dot_general | solution.py:75
  370.3 108.7 %all-gather.32.cloned.1.call-done = bf16[1,4096,2304]{1,2,0:T(8,128)(2,1)} async-done(((bf16[1,4096,576]{1,2,0:T(8,128)(2,1)}), bf16[1,4096,2304]{1,2,0:T(8,128)(2,1)}) %all-gather.32.cloned.1.call-update) | async-done | bytes 18874384 | tf_op jit(solution)/shard_map/all_gather | solution.py:72
  479.0 11.3 %fusion.35 = f32[256,2304]{1,0:T(8,128)} fusion(f32[256,2304]{1,0:T(8,128)} %fusion.6, bf16[256,4096]{1,0:T(8,128)(2,1)S(1)} %broadcast_select_fusion, bf16[1,4096,2304]{1,2,0:T(8,128)(2,1)} %all-gather.32.cloned.1.call-done), kind=kOutput, calls=%fused_computation.31 | convolution fusion | flops 4832428032 | bytes 25690112 | tf_op jit(solution)/shard_map/dot_general | solution.py:76
  490.3 61.0 %all-gather.36.cloned.1.call-done = bf16[1,2304,2304]{2,1,0:T(8,128)(2,1)} async-done(((bf16[1,576,2304]{2,1,0:T(8,128)(2,1)}), bf16[1,2304,2304]{2,1,0:T(8,128)(2,1)}) %all-gather.36.cloned.1.call-update) | async-done | bytes 10616848 | tf_op jit(solution)/shard_map/all_gather | solution.py:57
  551.4 72.5 %all-gather.38.cloned.1.call-done = bf16[1,2304,2304]{1,2,0:T(8,128)(2,1)} async-done(((bf16[1,2304,576]{1,2,0:T(8,128)(2,1)}), bf16[1,2304,2304]{1,2,0:T(8,128)(2,1)}) %all-gather.38.cloned.1.call-update) | async-done | bytes 10616848 | tf_op jit(solution)/shard_map/all_gather | solution.py:79
  623.9 16.2 %fusion.32 = f32[256,2304]{1,0:T(8,128)} fusion(f32[256,2304]{1,0:T(8,128)} %fusion.35, bf16[1,2304,2304]{1,2,0:T(8,128)(2,1)} %all-gather.38.cloned.1.call-done, f32[256,2304]{1,0:T(8,128)} %fusion.50, bf16[256,2304]{0,1:T(8,128)(2,1)} %fusion.43, bf16[1,2304,2304]{2,1,0:T(8,128)(2,1)} %all-gather.36.cloned.1.call-done), kind=kOutput, calls=%fused_computation.30 | convolution fusion | flops 5437587456 | bytes 29491200 | tf_op jit(solution)/shard_map/dot_general | solution.py:77
  641.4 165.5 %all-gather.40.cloned.1.call-done = f32[1024,2304]{1,0:T(8,128)} async-done(((f32[256,2304]{1,0:T(8,128)}), f32[1024,2304]{1,0:T(8,128)}) %all-gather.40.cloned.1.call-update) | async-done | bytes 9437200 | tf_op jit(solution)/shard_map/all_gather | solution.py:12
  811.4 12.8 %fusion.22 = bf16[256,4096]{1,0:T(8,128)(2,1)S(1)} fusion(bf16[256,2304]{1,0:T(8,128)(2,1)S(1)} %reduce_sum.28, bf16[1,4096,2304]{1,2,0:T(8,128)(2,1)} %all-gather.32.cloned.1.call-done), kind=kOutput, calls=%fused_computation.22 | convolution fusion | flops 4832886784 | bytes 22151168 | tf_op jit(solution)/shard_map/dot_general | solution.py:85
  825.6 48.2 %collective-permute-done.1 = bf16[256,4096]{1,0:T(8,128)(2,1)S(1)} collective-permute-done((bf16[256,4096]{1,0:T(8,128)(2,1)S(1)}, bf16[256,4096]{1,0:T(8,128)(2,1)S(1)}, u32[]{:S(2)}, u32[]{:S(2)}) %collective-permute-start.1) | collective-permute-done | bytes 2097184 | tf_op jit(solution)/shard_map/ppermute | solution.py:19
  873.7 18.3 %fusion.28 = bf16[256,4096]{1,0:T(8,128)(2,1)} fusion(f32[256,4096]{1,0:T(8,128)S(1)} %copy-done.5, bf16[256,4096]{1,0:T(8,128)(2,1)S(1)} %collective-permute-done.1, f32[32,8,32,128]{3,2,1,0:T(8,128)S(1)} %bitcast.95, bf16[256,2304]{1,0:T(8,128)(2,1)S(1)} %reduce_sum.28, bf16[1,4096,2304]{1,2,0:T(8,128)(2,1)} %all-gather.30.cloned.1.call-done), kind=kOutput, calls=%fused_computation.28 | convolution fusion | flops 4839178240 | bytes 32636928 | tf_op jit(solution)/shard_map/dot_general | solution.py:84
  897.0 27.4 %all-to-all-done = bf16[256,4,576]{0,2,1:T(8,128)(2,1)S(1)} async-done(((bf16[256,4,576]{0,2,1:T(8,128)(2,1)}), bf16[256,4,576]{0,2,1:T(8,128)(2,1)S(1)}, u32[]{:S(2)}, u32[]{:S(2)}) %all-to-all-start) | async-done | bytes 1179680 | tf_op jit(solution)/shard_map/all_to_all | solution.py:90
  928.4 19.8 %all-to-all-done.1 = bf16[256,4,576]{0,2,1:T(8,128)(2,1)S(1)} async-done(((bf16[256,4,576]{0,2,1:T(8,128)(2,1)}), bf16[256,4,576]{0,2,1:T(8,128)(2,1)S(1)}, u32[]{:S(2)}, u32[]{:S(2)}) %all-to-all-start.1) | async-done | bytes 1179680 | tf_op jit(solution)/shard_map/all_to_all | solution.py:91
  948.4 10.9 %multiply_bitcast_fusion = f32[1,4096,576]{1,2,0:T(8,128)} fusion(bf16[1024,576]{0,1:T(8,128)(2,1)S(1)} %bitcast.100, bf16[1024,4096]{1,0:T(8,128)(2,1)} %all-gather.24.cloned.1.call-done), kind=kOutput, calls=%fused_computation.17 | convolution fusion | flops 4834197504 | bytes 19005440 | tf_op jit(solution)/shard_map/dot_general | solution.py:100
  959.3 12.1 %multiply_bitcast_fusion.1 = f32[1,4096,576]{1,2,0:T(8,128)} fusion(bf16[1024,576]{0,1:T(8,128)(2,1)S(1)} %bitcast.101, bf16[1024,4096]{1,0:T(8,128)(2,1)} %all-gather.22.cloned.1.call-done), kind=kOutput, calls=%fused_computation.18 | convolution fusion | flops 4834197504 | bytes 19005440 | tf_op jit(solution)/shard_map/dot_general | solution.py:99
  971.4 39.0 %all-gather.20.cloned.1.call-done = bf16[1024,4096]{1,0:T(8,128)(2,1)} async-done(((bf16[256,4096]{1,0:T(8,128)(2,1)}), bf16[1024,4096]{1,0:T(8,128)(2,1)}) %all-gather.20.cloned.1.call-update) | async-done | bytes 8388624 | tf_op jit(solution)/shard_map/all_gather | solution.py:96
  1010.5 5.3 convert_reduce_fusion
  1016.2 7.5 convolution_bitcast_fusion
  (64 shorter events, 34.0 us)
Async XLA Ops:
  7.2 35.6 %all-gather.26.cloned.1.call-start = ((), (), s32[]{:S(2)}) async-start(), calls=%async_computation.5 | async-start | bytes 1474560 | tf_op jit(solution)/shard_map/all_gather | solution.py:44
  7.9 155.7 %all-gather.28.cloned.1.call-start = ((), (), s32[]{:S(2)}) async-start(), calls=%async_computation.6 | async-start | bytes 23592960 | tf_op jit(solution)/shard_map/all_gather | solution.py:58
  8.6 227.4 %all-gather.34.cloned.1.call-start = ((), (), s32[]{:S(2)}) async-start(), calls=%async_computation.9 | async-start | bytes 13271040 | tf_op jit(solution)/shard_map/all_gather | solution.py:56
  9.4 348.2 %all-gather.30.cloned.1.call-start = ((), (), s32[]{:S(2)}) async-start(), calls=%async_computation.7 | async-start | bytes 23592960 | tf_op jit(solution)/shard_map/all_gather | solution.py:71
  10.0 469.0 %all-gather.32.cloned.1.call-start = ((), (), s32[]{:S(2)}) async-start(), calls=%async_computation.8 | async-start | bytes 23592960 | tf_op jit(solution)/shard_map/all_gather | solution.py:72
  10.6 2.7 copy-start.7
  10.6 17.0 %copy-start.8 = (s32[1,2,32]{2,1,0:T(2,128)S(1)}, s32[1,2,32]{2,1,0:T(2,128)}, u32[]{:S(2)}) copy-start(s32[1,2,32]{2,1,0:T(2,128)} %param.14) | copy-start | bytes 772
  10.6 540.8 %all-gather.36.cloned.1.call-start = ((), (), s32[]{:S(2)}) async-start(), calls=%async_computation.10 | async-start | bytes 13271040 | tf_op jit(solution)/shard_map/all_gather | solution.py:57
  11.2 612.7 %all-gather.38.cloned.1.call-start = ((), (), s32[]{:S(2)}) async-start(), calls=%async_computation.11 | async-start | bytes 13271040 | tf_op jit(solution)/shard_map/all_gather | solution.py:79
  11.9 795.1 %all-gather.40.cloned.1.call-start = ((), (), s32[]{:S(2)}) async-start(), calls=%async_computation.12 | async-start | bytes 11796480 | tf_op jit(solution)/shard_map/all_gather | solution.py:12
  47.0 117.1 %copy-start.6 = (f32[1,4096]{1,0:T(1,128)S(1)}, f32[1,4096]{1,0:T(1,128)}, u32[]{:S(2)}) copy-start(f32[1,4096]{1,0:T(1,128)} %param.19) | copy-start | bytes 49156
  164.2 16.1 %copy-start = (f32[2,128,32,128]{3,2,1,0:T(8,128)}, f32[2,128,32,128]{3,2,1,0:T(8,128)S(1)}, u32[]{:S(2)}) copy-start(f32[2,128,32,128]{3,2,1,0:T(8,128)S(1)} %broadcast_in_dim.20) | copy-start | bytes 12582916
  180.3 177.3 %copy-start.2 = (bf16[256,4096]{1,0:T(8,128)(2,1)}, bf16[256,4096]{1,0:T(8,128)(2,1)S(1)}, u32[]{:S(2)}) copy-start(bf16[256,4096]{1,0:T(8,128)(2,1)S(1)} %get-tuple-element.4) | copy-start | bytes 6291460
  180.3 187.7 %collective-permute-start = (bf16[256,4096]{1,0:T(8,128)(2,1)S(1)}, bf16[256,4096]{1,0:T(8,128)(2,1)}, u32[]{:S(2)}, u32[]{:S(2)}) collective-permute-start(bf16[256,4096]{1,0:T(8,128)(2,1)S(1)} %get-tuple-element.4), channel_id=1, source_target_pairs={{0,16},{1,17},{2,18},{3,19},{4,20},{5,21},{6,22},{7,23},{8,24},{9,... | collective-permute-start | bytes 6291464 | tf_op jit(solution)/shard_map/ppermute | solution.py:19
  370.3 120.1 %copy-start.3 = (bf16[256,4096]{1,0:T(8,128)(2,1)}, bf16[256,4096]{1,0:T(8,128)(2,1)S(1)}, u32[]{:S(2)}) copy-start(bf16[256,4096]{1,0:T(8,128)(2,1)S(1)} %broadcast_select_fusion) | copy-start | bytes 6291460
  640.1 308.3 %all-gather.24.cloned.1.call-start = ((), (), s32[]{:S(2)}) async-start(), calls=%async_computation.4 | async-start | bytes 10485760 | tf_op jit(solution)/shard_map/all_gather | solution.py:94
  640.8 318.5 %all-gather.22.cloned.1.call-start = ((), (), s32[]{:S(2)}) async-start(), calls=%async_computation.3 | async-start | bytes 10485760 | tf_op jit(solution)/shard_map/all_gather | solution.py:93
  641.4 369.1 %all-gather.20.cloned.1.call-start = ((), (), s32[]{:S(2)}) async-start(), calls=%async_computation.2 | async-start | bytes 10485760 | tf_op jit(solution)/shard_map/all_gather | solution.py:96
  811.4 62.3 %copy-start.1 = (f32[2,128,32,128]{3,2,1,0:T(8,128)S(1)}, f32[2,128,32,128]{3,2,1,0:T(8,128)}, u32[]{:S(2)}) copy-start(f32[2,128,32,128]{3,2,1,0:T(8,128)} %copy-done) | copy-start | bytes 12582916
  811.4 62.3 %copy-start.5 = (f32[256,4096]{1,0:T(8,128)S(1)}, f32[256,4096]{1,0:T(8,128)}, u32[]{:S(2)}) copy-start(f32[256,4096]{1,0:T(8,128)} %get-tuple-element.5) | copy-start | bytes 12582916
  824.3 49.5 %collective-permute-start.1 = (bf16[256,4096]{1,0:T(8,128)(2,1)S(1)}, bf16[256,4096]{1,0:T(8,128)(2,1)S(1)}, u32[]{:S(2)}, u32[]{:S(2)}) collective-permute-start(bf16[256,4096]{1,0:T(8,128)(2,1)S(1)} %fusion.22), channel_id=1, source_target_pairs={{16,0},{17,1},{18,2},{19,3},{20,4},{21,5},{22,6},{23,7},{24,8},{25... | collective-permute-start | bytes 6291464 | tf_op jit(solution)/shard_map/ppermute | solution.py:19
  892.1 32.4 %all-to-all-start = ((bf16[256,4,576]{0,2,1:T(8,128)(2,1)}), bf16[256,4,576]{0,2,1:T(8,128)(2,1)S(1)}, u32[]{:S(2)}, u32[]{:S(2)}) async-start(bf16[256,4,576]{0,2,1:T(8,128)(2,1)} %bitcast.3), calls=%async_computation | async-start | bytes 2359296 | tf_op jit(solution)/shard_map/all_to_all | solution.py:90
  924.5 23.8 %all-to-all-start.1 = ((bf16[256,4,576]{0,2,1:T(8,128)(2,1)}), bf16[256,4,576]{0,2,1:T(8,128)(2,1)S(1)}, u32[]{:S(2)}, u32[]{:S(2)}) async-start(bf16[256,4,576]{0,2,1:T(8,128)(2,1)} %bitcast.16), calls=%async_computation.1 | async-start | bytes 2359296 | tf_op jit(solution)/shard_map/all_to_all | solution.py:91
  1010.5 5.8 copy-start.4
  (1 other events, 1.4 us)
Sparse Core Ops, SparseCore 0:
  9.5 33.1 all-gather.25
  44.3 119.2 all-gather.27
  165.1 70.9 all-gather.33
  237.5 119.9 all-gather.29
  359.0 119.9 all-gather.31
  480.4 70.9 all-gather.35
  552.9 70.9 all-gather.37
  640.2 166.7 all-gather.39
  808.5 56.4 all-gather.23
  866.4 75.3 all-gather.21
  944.0 66.4 all-gather.19
